TPU v7x, 32 devices: a whole 2x2x4 slice. The times are simulated.
32 devices in a mesh: band: 2 (over x), feed: 16 (over z, y, core).
Axes of the slice: x: 2, y: 2, z: 4, core: 2. Of those that a mesh axis runs over, the one named last changes fastest.
Arguments:
- samples: int32 [8192, 16, 519], P(('band', 'feed')), parts along dimension 0, may hold values from 0 to 255
- gains: int32 [2, 32, 4096], P(None, 'band', 'feed'), parts along dimension 1, may hold values from -2048 to 2047
- feed_slot: int32 [4096], replicated, may hold values from 0 to 4095, each once
Outputs:
- visibility: float32 [8192, 2, 4096], P(('band', 'feed')), parts along dimension 0
There are 2 independent parts, one for each index of `band`. A program takes and returns all parts, laid end to end along the dimension named above; an argument that names none is the same for every part. Nothing has to cross between parts.
Inputs may be any that keep to these rules, and one draw needn't show every extreme that they name: `samples`: each word is 16 times the in-phase level plus the quadrature level, both offset by 8. `feed_slot`: every slot appears once.
All inputs are finite; a program needn't handle non-finite values.
Results may differ from a plain program's by a relative error of at most 0.0026.
Values may be sent and summed in bfloat16 or wider, within the bound.
A program may use at most 128 MiB of HBM per device.

v0:
```python
import functools
import math

import jax
import jax.numpy as jnp
import numpy as np
from jax import lax
from jax.experimental import pallas as pl
from jax.experimental.pallas import tpu as pltpu
from jax.sharding import PartitionSpec as P

CH = 16
TAPS = 8
SPECTRA = 512
ROWS = 256
SHARES = (4, 5, 5, 2)
SPAN = 32
TILE = 512
TERMS = 3
LANES = 128


def filter_bank():
    length = TAPS * CH
    place = np.arange(length, dtype=np.float64)
    window = 0.5 - 0.5 * np.cos(2.0 * math.pi * place / (length - 1))
    taps = (np.sinc((place - 0.5 * (length - 1)) / CH) * window).reshape(TAPS, CH)
    index = np.arange(CH)
    angle = (index[:, None] * index[None, :] % CH) * (2.0 * math.pi / CH)
    cosine = np.cos(angle) / math.sqrt(CH)
    sine = np.sin(angle) / math.sqrt(CH)
    table = np.stack([np.stack([cosine, sine], 1), np.stack([-sine, cosine], 1)], 0)
    bank = table[:, :, None, :, :] * taps[None, None, :, None, :]
    bank = 0.125 * bank.reshape(2 * CH, TAPS * 2 * CH)
    terms = []
    for _ in range(TERMS):
        term = bank.astype(jnp.bfloat16)
        terms.append(term)
        bank = bank - term.astype(np.float64)
    return np.concatenate(terms, 0)


def unpack(words):
    inphase = ((words >> 4) - 8).astype(jnp.float32).astype(jnp.bfloat16)
    quadrature = ((words & 15) - 8).astype(jnp.float32).astype(jnp.bfloat16)
    return jnp.concatenate([inphase, quadrature], axis=0)


def pick(moved_ref, columns):
    sources, _, width = moved_ref.shape
    total = None
    for source in range(sources):
        place = lax.broadcasted_iota(jnp.int32, (width, columns.shape[1]), 0) + source * width
        hot = jnp.where(place == columns, 1.0, 0.0).astype(jnp.bfloat16)
        part = jnp.dot(moved_ref[source], hot, preferred_element_type=jnp.float32)
        total = part if total is None else total + part
    return total


def set_left(left, moved_ref, columns, scale):
    depth = moved_ref.shape[1]
    feed_rows = jnp.transpose(pick(moved_ref, columns)) * scale
    real, imag = feed_rows[:, : depth // 2], feed_rows[:, depth // 2 :]
    left[0, :, :depth] = jnp.concatenate([real, imag], axis=1).astype(jnp.bfloat16)
    left[1, :, :depth] = jnp.concatenate([imag, -real], axis=1).astype(jnp.bfloat16)


def exchange_kernel(counts, groups, scale, bank_ref, words_hbm, gains_ref, slot_ref, own_ref, *refs):
    chunks = len(counts)
    last_hbm, total_hbm = refs[:2]
    words_bufs = refs[2 : 2 + chunks]
    send_bufs = refs[2 + chunks : 2 + 2 * chunks]
    hold_bufs = refs[2 + 2 * chunks : 1 + 3 * chunks]
    voltage, rows, total, left, word_sem, own_sem, total_sem, send_sem, recv_sem = refs[1 + 3 * chunks :]
    targets = hold_bufs + (last_hbm,)
    me = lax.axis_index("feed")
    size = lax.axis_size("feed")
    inputs = send_bufs[0].shape[2]
    bank = bank_ref[...]
    gain = gains_ref[...].astype(jnp.float32) * (1.0 / 2048.0)

    barrier = pltpu.get_barrier_semaphore()

    def greet(d, carry):
        pl.semaphore_signal(
            barrier, inc=1, device_id={"feed": (me + d) % size}, device_id_type=pl.DeviceIdType.MESH
        )
        return carry

    lax.fori_loop(1, size, greet, 0)

    def word_copy(k):
        source = words_hbm.at[pl.ds(sum(counts[:k]), counts[k] + TAPS - 1)]
        return pltpu.make_async_copy(source, words_bufs[k], word_sem.at[k])

    def own_copy(k):
        return pltpu.make_async_copy(send_bufs[k].at[me // groups], targets[k].at[me], own_sem.at[k])

    def remote(k, d):
        there = (me + d) % size
        return pltpu.make_async_remote_copy(
            src_ref=send_bufs[k].at[there // groups],
            dst_ref=targets[k].at[me],
            send_sem=send_sem.at[k, d],
            recv_sem=recv_sem.at[k, d],
            device_id={"feed": there},
            device_id_type=pl.DeviceIdType.MESH,
        )

    def channelize(k):
        words, out = words_bufs[k], send_bufs[k]
        count = counts[k]

        def block(i, carry):
            base = i * SPAN
            for m in range(SPAN + TAPS - 1):
                voltage[m * 2 * CH : (m + 1) * 2 * CH, :] = unpack(words[base + m])
            for s in range(SPAN):
                window = voltage[s * 2 * CH : (s + TAPS) * 2 * CH, :]
                parts = jnp.dot(bank, window, preferred_element_type=jnp.float32)
                whole = parts[: 2 * CH]
                for term in range(1, TERMS):
                    whole = whole + parts[2 * CH * term : 2 * CH * (term + 1)]
                real, imag = whole[:CH], whole[CH:]
                upper = gain[0] * real - gain[1] * imag
                lower = gain[0] * imag + gain[1] * real
                for lane in range(rows.shape[1]):
                    place = slice(lane * LANES, (lane + 1) * LANES)
                    rows[0, lane, s * CH : (s + 1) * CH, :] = upper[:, place]
                    rows[1, lane, s * CH : (s + 1) * CH, :] = lower[:, place]
            for c in range(CH):
                for part in range(2):
                    where = pl.ds(pl.multiple_of(part * count + base, SPAN), SPAN)
                    for lane in range(rows.shape[1]):
                        width = min(LANES, inputs - lane * LANES)
                        piece = rows[part, lane, pl.ds(c, SPAN, stride=CH), :]
                        out[c, where, lane * LANES : lane * LANES + width] = piece[:, :width].astype(
                            jnp.bfloat16
                        )
            return carry

        lax.fori_loop(0, count // SPAN, block, 0)

    def send(k):
        def one(d, carry):
            remote(k, d).start()
            return carry

        lax.fori_loop(1, size, one, 0)
        own_copy(k).start()

    def arrive(k):
        def one(d, carry):
            remote(k, d).wait_recv()
            return carry

        own_copy(k).wait()
        lax.fori_loop(1, size, one, 0)

    def drain(k):
        def one(d, carry):
            remote(k, d).wait_send()
            return carry

        lax.fori_loop(1, size, one, 0)

    for k in range(chunks):
        word_copy(k).start()
    for k in range(chunks):
        word_copy(k).wait()
        channelize(k)
        if k == 0:
            pl.semaphore_wait(barrier, size - 1)
        send(k)

    feeds = slot_ref.shape[1]
    tile = min(TILE, feeds)
    for k in range(chunks - 1):
        arrive(k)
        depth = 2 * counts[k]
        set_left(left, hold_bufs[k], own_ref[...], scale)

        def columns(j, carry, k=k, depth=depth):
            where = pl.ds(pl.multiple_of(j * tile, tile), tile)
            ordered = pick(hold_bufs[k], slot_ref[:, where]).astype(jnp.bfloat16)
            for part in range(2):
                product = jnp.dot(left[part, :, :depth], ordered, preferred_element_type=jnp.float32)
                if k:
                    product = product + total[part, :, where]
                total[part, :, where] = product
            return carry

        lax.fori_loop(0, feeds // tile, columns, 0)
    total_copy = pltpu.make_async_copy(total, total_hbm, total_sem)
    total_copy.start()
    arrive(chunks - 1)
    for k in range(chunks):
        drain(k)
    total_copy.wait()


def exchange(words, gains, feed_slot, own, counts, inputs, groups, scale):
    size = CH * groups
    feeds = feed_slot.shape[0]
    wide = words.shape[2]
    bank = jnp.asarray(filter_bank())
    held = [jax.ShapeDtypeStruct((size, 2 * count, inputs), jnp.bfloat16) for count in counts]
    memory = pl.BlockSpec(memory_space=pltpu.VMEM)
    anywhere = pl.BlockSpec(memory_space=pl.ANY)
    chunks = len(counts)
    return pl.pallas_call(
        functools.partial(exchange_kernel, counts, groups, scale),
        out_shape=(held[-1], jax.ShapeDtypeStruct((2, ROWS, feeds), jnp.float32)),
        in_specs=[memory, anywhere, memory, memory, memory],
        out_specs=(anywhere, anywhere),
        scratch_shapes=[pltpu.VMEM((count + TAPS - 1, CH, wide), jnp.int32) for count in counts]
        + [pltpu.VMEM((CH, 2 * count, inputs), jnp.bfloat16) for count in counts]
        + [pltpu.VMEM(one.shape, one.dtype) for one in held[:-1]]
        + [
            pltpu.VMEM(((SPAN + TAPS) * 2 * CH, wide), jnp.bfloat16),
            pltpu.VMEM((2, wide // LANES, SPAN * CH, LANES), jnp.float32),
            pltpu.VMEM((2, ROWS, feeds), jnp.float32),
            pltpu.VMEM((2, ROWS, 2 * max(counts)), jnp.bfloat16),
            pltpu.SemaphoreType.DMA((chunks,)),
            pltpu.SemaphoreType.DMA((chunks,)),
            pltpu.SemaphoreType.DMA,
            pltpu.SemaphoreType.DMA((chunks, size)),
            pltpu.SemaphoreType.DMA((chunks, size)),
        ],
        compiler_params=pltpu.CompilerParams(
            collective_id=0, has_side_effects=True, vmem_limit_bytes=60 * 2**20
        ),
    )(bank, words, gains, feed_slot[None], own[None])


def finish_kernel(scale, moved_ref, slot_ref, own_ref, total_ref, out_ref, left):
    @pl.when(pl.program_id(0) == 0)
    def _():
        set_left(left, moved_ref, own_ref[...], scale)

    ordered = pick(moved_ref, slot_ref[...]).astype(jnp.bfloat16)
    for part in range(2):
        product = jnp.dot(left[part], ordered, preferred_element_type=jnp.float32)
        out_ref[:, part, :] = product + total_ref[part]


def finish(moved, feed_slot, own, total, scale):
    feeds = feed_slot.shape[0]
    tile = min(TILE, feeds)
    return pl.pallas_call(
        functools.partial(finish_kernel, scale),
        out_shape=jax.ShapeDtypeStruct((ROWS, 2, feeds), jnp.float32),
        grid=(feeds // tile,),
        in_specs=[
            pl.BlockSpec(moved.shape, lambda j: (0, 0, 0)),
            pl.BlockSpec((1, tile), lambda j: (0, j)),
            pl.BlockSpec((1, ROWS), lambda j: (0, 0)),
            pl.BlockSpec((2, ROWS, tile), lambda j: (0, 0, j)),
        ],
        out_specs=pl.BlockSpec((ROWS, 2, tile), lambda j: (0, 0, j)),
        scratch_shapes=[pltpu.VMEM((2, ROWS, moved.shape[1]), jnp.bfloat16)],
    )(moved, feed_slot[None], own[None], total)


def body(samples, gains, feed_slot):
    groups = lax.axis_size("feed") // CH
    first = lax.axis_index("feed") % groups * ROWS
    inputs = samples.shape[0]
    spectra = samples.shape[2] - TAPS + 1
    counts = tuple(spectra * share // sum(SHARES) for share in SHARES)
    words = jnp.transpose(samples, (2, 1, 0))
    spare = -inputs % LANES
    if spare:
        words = jnp.pad(words, ((0, 0), (0, 0), (0, spare)))
        gains = jnp.pad(gains, ((0, 0), (0, 0), (0, spare)))
    own = lax.dynamic_slice_in_dim(feed_slot, first, ROWS, 0)
    scale = 1.0 / spectra
    moved, total = exchange(words, gains, feed_slot, own, counts, inputs, groups, scale)
    return finish(moved, feed_slot, own, total, scale)


def solution(mesh):
    return jax.shard_map(
        body,
        mesh=mesh,
        in_specs=(P(("band", "feed"), None, None), P(None, "band", "feed"), P()),
        out_specs=P(("band", "feed"), None, None),
        check_vma=False,
    )
```

profile of v0, /device:TPU:13, one launch (start us, length us, event | category | flops | bytes accessed | tf_op | source)
XLA Modules:
  0.0 215.0 jit_solution(1317333146116813871)
XLA Ops:
  0.0 1.3 dynamic_slice.3
  1.3 199.9 %shard_map.46 = (bf16[16,128,256]{2,1,0:T(8,128)(2,1)}, f32[2,256,4096]{2,1,0:T(8,128)}) custom-call(bf16[96,256]{1,0:T(8,128)(2,1)} %constant.20.clone.bank_ref, s32[519,16,256]{2,1,0:T(8,128)} %bitcast.3, s32[2,16,256]{2,1,0:T(8,128)} %gains_ref.1, s32[1,4096]{1,0:T(1,128)} %bitcast.4, s32[1,256]{1,0:T(1,128)} %bitcast.6), custom_call_target="tpu_custom_call" | custom-call | tf_op jit(solution)/shard_map/pallas_call | solution.py:211
  201.2 13.8 %shard_map.47 = f32[256,2,4096]{2,1,0:T(2,128)} custom-call(bf16[16,128,256]{2,1,0:T(8,128)(2,1)} %get-tuple-element.7.moved_ref, s32[1,4096]{1,0:T(1,128)} %bitcast.5, s32[1,256]{1,0:T(1,128)} %bitcast.7, f32[2,256,4096]{2,1,0:T(8,128)} %get-tuple-element.8.total_ref), custom_call_target="tpu_custom_call" | custom-call | tf_op jit(solution)/shard_map/pallas_call | solution.py:250
where the time goes:
time: 215 us
  Pallas kernels  214 us (100%)
    pallas_call x1, Pallas kernels, exchange(): pl.pallas_call(functools.partial(exchange_kernel, counts, groups, scale),...  200 us
    pallas_call x1, Pallas kernels, finish(): pl.pallas_call(functools.partial(finish_kernel, scale), out_shape=jax.Sha...  13.8 us

commit v1 on v0

--- a/solution.py
+++ b/solution.py
@@ -14,6 +14,7 @@
 SPECTRA = 512
 ROWS = 256
 SHARES = (4, 5, 5, 2)
+SPLIT_SHARES = (2, 3, 2, 1)
 SPAN = 32
 TILE = 512
 TERMS = 3
@@ -46,23 +47,61 @@
     return jnp.concatenate([inphase, quadrature], axis=0)
 
 
-def pick(moved_ref, columns):
+def pick(moved_ref, columns, first=0):
     sources, _, width = moved_ref.shape
     total = None
     for source in range(sources):
-        place = lax.broadcasted_iota(jnp.int32, (width, columns.shape[1]), 0) + source * width
+        place = lax.broadcasted_iota(jnp.int32, (width, columns.shape[1]), 0) + (source * width + first)
         hot = jnp.where(place == columns, 1.0, 0.0).astype(jnp.bfloat16)
         part = jnp.dot(moved_ref[source], hot, preferred_element_type=jnp.float32)
         total = part if total is None else total + part
     return total
 
 
-def set_left(left, moved_ref, columns, scale):
-    depth = moved_ref.shape[1]
-    feed_rows = jnp.transpose(pick(moved_ref, columns)) * scale
+def put_left(left, picked, scale):
+    depth = picked.shape[0]
+    feed_rows = jnp.transpose(picked) * scale
     real, imag = feed_rows[:, : depth // 2], feed_rows[:, depth // 2 :]
     left[0, :, :depth] = jnp.concatenate([real, imag], axis=1).astype(jnp.bfloat16)
     left[1, :, :depth] = jnp.concatenate([imag, -real], axis=1).astype(jnp.bfloat16)
+
+
+def set_left(left, moved_ref, columns, scale):
+    put_left(left, pick(moved_ref, columns), scale)
+
+
+def channelize(count, bank, gain, words, out, voltage, rows):
+    inputs = out.shape[2]
+
+    def block(i, carry):
+        base = i * SPAN
+        for m in range(SPAN + TAPS - 1):
+            voltage[m * 2 * CH : (m + 1) * 2 * CH, :] = unpack(words[base + m])
+        for s in range(SPAN):
+            window = voltage[s * 2 * CH : (s + TAPS) * 2 * CH, :]
+            parts = jnp.dot(bank, window, preferred_element_type=jnp.float32)
+            whole = parts[: 2 * CH]
+            for term in range(1, TERMS):
+                whole = whole + parts[2 * CH * term : 2 * CH * (term + 1)]
+            real, imag = whole[:CH], whole[CH:]
+            upper = gain[0] * real - gain[1] * imag
+            lower = gain[0] * imag + gain[1] * real
+            for lane in range(rows.shape[1]):
+                place = slice(lane * LANES, (lane + 1) * LANES)
+                rows[0, lane, s * CH : (s + 1) * CH, :] = upper[:, place]
+                rows[1, lane, s * CH : (s + 1) * CH, :] = lower[:, place]
+        for c in range(CH):
+            for part in range(2):
+                where = pl.ds(pl.multiple_of(part * count + base, SPAN), SPAN)
+                for lane in range(rows.shape[1]):
+                    width = min(LANES, inputs - lane * LANES)
+                    piece = rows[part, lane, pl.ds(c, SPAN, stride=CH), :]
+                    out[c, where, lane * LANES : lane * LANES + width] = piece[:, :width].astype(
+                        jnp.bfloat16
+                    )
+        return carry
+
+    lax.fori_loop(0, count // SPAN, block, 0)
 
 
 def exchange_kernel(counts, groups, scale, bank_ref, words_hbm, gains_ref, slot_ref, own_ref, *refs):
@@ -75,7 +114,6 @@
     targets = hold_bufs + (last_hbm,)
     me = lax.axis_index("feed")
     size = lax.axis_size("feed")
-    inputs = send_bufs[0].shape[2]
     bank = bank_ref[...]
     gain = gains_ref[...].astype(jnp.float32) * (1.0 / 2048.0)
 
@@ -107,40 +145,6 @@
             device_id_type=pl.DeviceIdType.MESH,
         )
 
-    def channelize(k):
-        words, out = words_bufs[k], send_bufs[k]
-        count = counts[k]
-
-        def block(i, carry):
-            base = i * SPAN
-            for m in range(SPAN + TAPS - 1):
-                voltage[m * 2 * CH : (m + 1) * 2 * CH, :] = unpack(words[base + m])
-            for s in range(SPAN):
-                window = voltage[s * 2 * CH : (s + TAPS) * 2 * CH, :]
-                parts = jnp.dot(bank, window, preferred_element_type=jnp.float32)
-                whole = parts[: 2 * CH]
-                for term in range(1, TERMS):
-                    whole = whole + parts[2 * CH * term : 2 * CH * (term + 1)]
-                real, imag = whole[:CH], whole[CH:]
-                upper = gain[0] * real - gain[1] * imag
-                lower = gain[0] * imag + gain[1] * real
-                for lane in range(rows.shape[1]):
-                    place = slice(lane * LANES, (lane + 1) * LANES)
-                    rows[0, lane, s * CH : (s + 1) * CH, :] = upper[:, place]
-                    rows[1, lane, s * CH : (s + 1) * CH, :] = lower[:, place]
-            for c in range(CH):
-                for part in range(2):
-                    where = pl.ds(pl.multiple_of(part * count + base, SPAN), SPAN)
-                    for lane in range(rows.shape[1]):
-                        width = min(LANES, inputs - lane * LANES)
-                        piece = rows[part, lane, pl.ds(c, SPAN, stride=CH), :]
-                        out[c, where, lane * LANES : lane * LANES + width] = piece[:, :width].astype(
-                            jnp.bfloat16
-                        )
-            return carry
-
-        lax.fori_loop(0, count // SPAN, block, 0)
-
     def send(k):
         def one(d, carry):
             remote(k, d).start()
@@ -168,7 +172,7 @@
         word_copy(k).start()
     for k in range(chunks):
         word_copy(k).wait()
-        channelize(k)
+        channelize(counts[k], bank, gain, words_bufs[k], send_bufs[k], voltage, rows)
         if k == 0:
             pl.semaphore_wait(barrier, size - 1)
         send(k)
@@ -244,11 +248,294 @@
         out_ref[:, part, :] = product + total_ref[part]
 
 
-def finish(moved, feed_slot, own, total, scale):
+def split_kernel(counts, scale, bank_ref, words_hbm, gains_ref, slot_ref, own_ref, *refs):
+    chunks = len(counts)
+    refs = list(refs)
+
+    def take(count):
+        taken = refs[:count]
+        del refs[:count]
+        return taken
+
+    last_hbm, total_hbm = take(2)
+    words_bufs = take(chunks)
+    send_bufs = take(chunks)
+    full_bufs = take(chunks - 1)
+    half_bufs = take(chunks)
+    give_bufs = take(chunks)
+    take_bufs = take(chunks)
+    lefts = take(chunks)
+    mine, theirs, voltage, rows, total, left = take(6)
+    word_sem, own_sem, total_sem, near_sems, cross_sems, row_sems, product_sems = refs
+    targets = full_bufs + [last_hbm]
+    me = lax.axis_index("feed")
+    size = lax.axis_size("feed")
+    half = size // 2
+    core = me % 2
+    base = me // half * half
+    away = half - base
+    spot = me - base
+    mate = away + spot + 1 - 2 * core
+    quarter = me // (size // 4)
+    inner = (quarter + 1) // 2 % 2
+    inputs = send_bufs[0].shape[2]
+    bank = bank_ref[...]
+    gain = gains_ref[...].astype(jnp.float32) * (1.0 / 2048.0)
+
+    barrier = pltpu.get_barrier_semaphore()
+
+    def greet(d, carry):
+        pl.semaphore_signal(
+            barrier, inc=1, device_id={"feed": (me + d) % size}, device_id_type=pl.DeviceIdType.MESH
+        )
+        return carry
+
+    lax.fori_loop(1, size, greet, 0)
+
+    def loop(first, last, step):
+        def one(i, carry):
+            step(i)
+            return carry
+
+        lax.fori_loop(first, last, one, 0)
+
+    def word_copy(k):
+        source = words_hbm.at[pl.ds(sum(counts[:k]), counts[k] + TAPS - 1)]
+        return pltpu.make_async_copy(source, words_bufs[k], word_sem.at[k])
+
+    def remote(source, target, sems, place, there):
+        send_sem, recv_sem = sems
+        return pltpu.make_async_remote_copy(
+            src_ref=source,
+            dst_ref=target,
+            send_sem=send_sem.at[place],
+            recv_sem=recv_sem.at[place],
+            device_id={"feed": there},
+            device_id_type=pl.DeviceIdType.MESH,
+        )
+
+    def channel(place):
+        odd = place % 2
+        return (base + place) * (1 - odd) + (away + place - 1) * odd
+
+    def near(k, d):
+        place = (spot + d) % half
+        return remote(
+            send_bufs[k].at[channel(place)], half_bufs[k].at[spot], near_sems, (k, d), base + place
+        )
+
+    def near_own(k):
+        return pltpu.make_async_copy(send_bufs[k].at[channel(spot)], half_bufs[k].at[spot], own_sem.at[0, k])
+
+    def far(k, i):
+        there = away + (spot + i) % half
+        return remote(send_bufs[k].at[there], targets[k].at[me], cross_sems, (k, half + i), there)
+
+    def close(k, i):
+        there = base + (spot + i) % half
+        return remote(send_bufs[k].at[there], targets[k].at[me], cross_sems, (k, i), there)
+
+    def cross_own(k):
+        return pltpu.make_async_copy(send_bufs[k].at[me], targets[k].at[me], own_sem.at[1, k])
+
+    def row_copy(k):
+        return remote(give_bufs[k], take_bufs[k], row_sems, k, mate)
+
+    def product_copy(j):
+        return remote(mine.at[j], theirs.at[j], product_sems, j, mate)
+
+    def send_near(k):
+        loop(1, half, lambda d: near(k, d).start())
+        near_own(k).start()
+
+    def arrive_near(k):
+        near_own(k).wait()
+        loop(1, half, lambda d: near(k, d).wait_recv())
+
+    def send_cross(k):
+        loop(0, half // 2, lambda q: far(k, 2 * q + 1 - core).start())
+        loop(core, half // 2, lambda q: close(k, 2 * q + 1 - core).start())
+
+    def drain(k):
+        loop(1, half, lambda d: near(k, d).wait_send())
+        loop(0, half // 2, lambda q: far(k, 2 * q + 1 - core).wait_send())
+        loop(core, half // 2, lambda q: close(k, 2 * q + 1 - core).wait_send())
+        row_copy(k).wait_send()
+
+    def arrive_cross(k):
+        cross_own(k).start()
+        cross_own(k).wait()
+        loop(1, half, lambda i: close(k, i).wait_recv())
+        loop(0, half, lambda i: far(k, i).wait_recv())
+
+    for k in range(chunks):
+        word_copy(k).start()
+    for k in range(chunks):
+        word_copy(k).wait()
+        channelize(counts[k], bank, gain, words_bufs[k], send_bufs[k], voltage, rows)
+        if k == 0:
+            pl.semaphore_wait(barrier, size - 1)
+        send_near(k)
+
+        @pl.when(inner == 1)
+        def _(k=k):
+            send_cross(k)
+
+    early = chunks // 2
+    for k in range(chunks):
+        arrive_near(k)
+        give_bufs[k][...] = pick(half_bufs[k], own_ref[...], base * inputs).astype(jnp.bfloat16)
+        row_copy(k).start()
+
+    @pl.when(inner == 0)
+    def _():
+        for k in range(early):
+            send_cross(k)
+
+    @pl.when((inner == 0) & (core == 0))
+    def _():
+        for k in range(early, chunks):
+            send_cross(k)
+
+    for k in range(chunks):
+        row_copy(k).wait_recv()
+        both = give_bufs[k][...].astype(jnp.float32) + take_bufs[k][...].astype(jnp.float32)
+        put_left(lefts[k], both, scale)
+
+    def multiply(j):
+        for part in range(2):
+            product = None
+            for k in range(chunks):
+                term = jnp.dot(lefts[k][part], half_bufs[k][j], preferred_element_type=jnp.float32)
+                product = term if product is None else product + term
+            mine[j, part * ROWS : (part + 1) * ROWS, :] = product.astype(jnp.bfloat16)
+
+        @pl.when(core == 1)
+        def _():
+            product_copy(j).start()
+
+    loop(0, half, multiply)
+
+    @pl.when((inner == 0) & (core == 1))
+    def _():
+        for k in range(early, chunks):
+            send_cross(k)
+
+    feeds = slot_ref.shape[1]
+    tile = min(TILE, feeds)
+
+    @pl.when(core == 0)
+    def _():
+        def place_mine(j):
+            where = pl.ds(pl.multiple_of(j * tile, tile), tile)
+            ordered = pick(mine, slot_ref[:, where], base * inputs)
+            total[0, :, where] = ordered[:ROWS]
+            total[1, :, where] = ordered[ROWS:]
+
+        def place_theirs(j):
+            where = pl.ds(pl.multiple_of(j * tile, tile), tile)
+            ordered = pick(theirs, slot_ref[:, where], away * inputs)
+            total[0, :, where] = total[0, :, where] + ordered[:ROWS]
+            total[1, :, where] = total[1, :, where] + ordered[ROWS:]
+
+        loop(0, feeds // tile, place_mine)
+        loop(0, half, lambda j: product_copy(j).wait_recv())
+        loop(0, feeds // tile, place_theirs)
+
+    @pl.when(core == 1)
+    def _():
+        for k in range(chunks - 1):
+            arrive_cross(k)
+            depth = 2 * counts[k]
+            set_left(left, full_bufs[k], own_ref[...], scale)
+
+            def columns(j, k=k, depth=depth):
+                where = pl.ds(pl.multiple_of(j * tile, tile), tile)
+                ordered = pick(full_bufs[k], slot_ref[:, where]).astype(jnp.bfloat16)
+                for part in range(2):
+                    product = jnp.dot(left[part, :, :depth], ordered, preferred_element_type=jnp.float32)
+                    if k:
+                        product = product + total[part, :, where]
+                    total[part, :, where] = product
+
+            loop(0, feeds // tile, columns)
+
+    total_copy = pltpu.make_async_copy(total, total_hbm, total_sem)
+    total_copy.start()
+
+    @pl.when(core == 1)
+    def _():
+        arrive_cross(chunks - 1)
+        loop(0, half, lambda j: product_copy(j).wait_send())
+
+    for k in range(chunks):
+        drain(k)
+    total_copy.wait()
+
+
+def split_exchange(words, gains, feed_slot, own, counts, inputs, scale):
+    size = CH
+    half = size // 2
+    feeds = feed_slot.shape[0]
+    wide = words.shape[2]
+    bank = jnp.asarray(filter_bank())
+    memory = pl.BlockSpec(memory_space=pltpu.VMEM)
+    anywhere = pl.BlockSpec(memory_space=pl.ANY)
+    chunks = len(counts)
+    half_type = jnp.bfloat16
+    return pl.pallas_call(
+        functools.partial(split_kernel, counts, scale),
+        out_shape=(
+            jax.ShapeDtypeStruct((size, 2 * counts[-1], inputs), jnp.bfloat16),
+            jax.ShapeDtypeStruct((2, ROWS, feeds), jnp.float32),
+        ),
+        in_specs=[memory, anywhere, memory, memory, memory],
+        out_specs=(anywhere, anywhere),
+        scratch_shapes=[pltpu.VMEM((count + TAPS - 1, CH, wide), jnp.int32) for count in counts]
+        + [pltpu.VMEM((CH, 2 * count, inputs), half_type) for count in counts]
+        + [pltpu.VMEM((size, 2 * count, inputs), half_type) for count in counts[:-1]]
+        + [pltpu.VMEM((half, 2 * count, inputs), half_type) for count in counts]
+        + [pltpu.VMEM((2 * count, ROWS), half_type) for count in counts] * 2
+        + [pltpu.VMEM((2, ROWS, 2 * count), half_type) for count in counts]
+        + [
+            pltpu.VMEM((half, 2 * ROWS, inputs), half_type),
+            pltpu.VMEM((half, 2 * ROWS, inputs), half_type),
+            pltpu.VMEM(((SPAN + TAPS) * 2 * CH, wide), half_type),
+            pltpu.VMEM((2, wide // LANES, SPAN * CH, LANES), jnp.float32),
+            pltpu.VMEM((2, ROWS, feeds), jnp.float32),
+            pltpu.VMEM((2, ROWS, 2 * max(counts)), half_type),
+            pltpu.SemaphoreType.DMA((chunks,)),
+            pltpu.SemaphoreType.DMA((2, chunks)),
+            pltpu.SemaphoreType.DMA,
+            (pltpu.SemaphoreType.DMA((chunks, half)),) * 2,
+            (pltpu.SemaphoreType.DMA((chunks, size)),) * 2,
+            (pltpu.SemaphoreType.DMA((chunks,)),) * 2,
+            (pltpu.SemaphoreType.DMA((half,)),) * 2,
+        ],
+        compiler_params=pltpu.CompilerParams(
+            collective_id=0, has_side_effects=True, vmem_limit_bytes=60 * 2**20
+        ),
+    )(bank, words, gains, feed_slot[None], own[None])
+
+
+def split_finish_kernel(scale, moved_ref, slot_ref, own_ref, total_ref, out_ref, left):
+    core = lax.axis_index("feed") % 2
+
+    @pl.when(core == 0)
+    def _():
+        for part in range(2):
+            out_ref[:, part, :] = total_ref[part]
+
+    @pl.when(core == 1)
+    def _():
+        finish_kernel(scale, moved_ref, slot_ref, own_ref, total_ref, out_ref, left)
+
+
+def finish(kernel, moved, feed_slot, own, total, scale):
     feeds = feed_slot.shape[0]
     tile = min(TILE, feeds)
     return pl.pallas_call(
-        functools.partial(finish_kernel, scale),
+        functools.partial(kernel, scale),
         out_shape=jax.ShapeDtypeStruct((ROWS, 2, feeds), jnp.float32),
         grid=(feeds // tile,),
         in_specs=[
@@ -267,7 +554,9 @@
     first = lax.axis_index("feed") % groups * ROWS
     inputs = samples.shape[0]
     spectra = samples.shape[2] - TAPS + 1
-    counts = tuple(spectra * share // sum(SHARES) for share in SHARES)
+    split = groups == 1 and inputs % LANES == 0
+    shares = SPLIT_SHARES if split else SHARES
+    counts = tuple(spectra * share // sum(shares) for share in shares)
     words = jnp.transpose(samples, (2, 1, 0))
     spare = -inputs % LANES
     if spare:
@@ -275,8 +564,11 @@
         gains = jnp.pad(gains, ((0, 0), (0, 0), (0, spare)))
     own = lax.dynamic_slice_in_dim(feed_slot, first, ROWS, 0)
     scale = 1.0 / spectra
+    if split:
+        moved, total = split_exchange(words, gains, feed_slot, own, counts, inputs, scale)
+        return finish(split_finish_kernel, moved, feed_slot, own, total, scale)
     moved, total = exchange(words, gains, feed_slot, own, counts, inputs, groups, scale)
-    return finish(moved, feed_slot, own, total, scale)
+    return finish(finish_kernel, moved, feed_slot, own, total, scale)
 
 
 def solution(mesh):

time: 215 us -> 233 us (1.084)
  the two profiles are of different devices: /device:TPU:13 before, /device:TPU:0 now
where the time goes in v1:
time: 233 us; the launch traced here: 229 us
  Pallas kernels  228 us (98%)
    pallas_call x1, Pallas kernels, split_exchange(): pl.pallas_call(functools.partial(split_kernel, counts, scale), out_shape=...  218 us
    pallas_call x1, Pallas kernels, finish(): pl.pallas_call(functools.partial(kernel, scale), out_shape=jax.ShapeDtype...  9.81 us

profile of v1, /device:TPU:0, one launch (start us, length us, event | category | flops | bytes accessed | tf_op | source)
XLA Modules:
  0.0 228.8 jit_solution(14738975155513699636)
XLA Ops:
  0.0 1.3 dynamic_slice.3
  1.3 217.7 %shard_map.46 = (bf16[16,128,256]{2,1,0:T(8,128)(2,1)}, f32[2,256,4096]{2,1,0:T(8,128)}) custom-call(bf16[96,256]{1,0:T(8,128)(2,1)} %constant.20.clone.bank_ref, s32[519,16,256]{2,1,0:T(8,128)} %bitcast.3, s32[2,16,256]{2,1,0:T(8,128)} %gains_ref.1, s32[1,4096]{1,0:T(1,128)} %bitcast.4, s32[1,256]{1,0:T(1,128)} %bitcast.6), custom_call_target="tpu_custom_call" | custom-call | tf_op jit(solution)/shard_map/pallas_call | solution.py:486
  219.0 9.8 %shard_map.47 = f32[256,2,4096]{2,1,0:T(2,128)} custom-call(bf16[16,128,256]{2,1,0:T(8,128)(2,1)} %get-tuple-element.7.moved_ref, s32[1,4096]{1,0:T(1,128)} %bitcast.5, s32[1,256]{1,0:T(1,128)} %bitcast.7, f32[2,256,4096]{2,1,0:T(8,128)} %get-tuple-element.8.total_ref), custom_call_target="tpu_custom_call" | custom-call | tf_op jit(solution)/shard_map/pallas_call | solution.py:537

commit v2 on v1

--- a/solution.py
+++ b/solution.py
@@ -19,6 +19,27 @@
 TILE = 512
 TERMS = 3
 LANES = 128
+ROWS_SENT, PRODUCTS_SENT = 100, 101
+
+
+def issue_plan():
+    kinds = ("straight", "across", "close")
+    chunks = range(len(SPLIT_SHARES))
+    last = chunks[-1]
+    plan = {}
+    for core in range(2):
+        inner = [(k, "straight", k) for k in chunks] + [(last, "across", k) for k in chunks]
+        inner += [(PRODUCTS_SENT if core else ROWS_SENT, "close", k) for k in chunks]
+        outer = []
+        for k in chunks:
+            stage = last if k < 2 - core else PRODUCTS_SENT if core else ROWS_SENT
+            outer += [(stage, kind, k) for kind in kinds]
+        plan[2 + core] = inner
+        plan[core] = outer
+    return plan
+
+
+ISSUE = issue_plan()
 
 
 def filter_bank():
@@ -352,9 +373,34 @@
         near_own(k).wait()
         loop(1, half, lambda d: near(k, d).wait_recv())
 
-    def send_cross(k):
-        loop(0, half // 2, lambda q: far(k, 2 * q + 1 - core).start())
+    plane = half // 2
+
+    def straight(k, q):
+        return far(k, (q * plane + spot % plane // 2 * 2 + 1 - spot + half) % half)
+
+    def across(k, q):
+        return far(k, (q * plane + (spot + 2) % plane // 2 * 2 + 1 - spot + half) % half)
+
+    def send_straight(k):
+        loop(0, 2, lambda q: straight(k, q).start())
+
+    def send_across(k):
+        loop(0, 2, lambda q: across(k, q).start())
+
+    def send_close(k):
         loop(core, half // 2, lambda q: close(k, 2 * q + 1 - core).start())
+
+    senders = {"straight": send_straight, "across": send_across, "close": send_close}
+
+    def issue(stage):
+        for place, plan in ISSUE.items():
+            steps = [step for step in plan if step[0] == stage]
+            if steps:
+
+                @pl.when((inner == place // 2) & (core == place % 2))
+                def _(steps=steps):
+                    for _, kind, k in steps:
+                        senders[kind](k)
 
     def drain(k):
         loop(1, half, lambda d: near(k, d).wait_send())
@@ -376,26 +422,14 @@
         if k == 0:
             pl.semaphore_wait(barrier, size - 1)
         send_near(k)
-
-        @pl.when(inner == 1)
-        def _(k=k):
-            send_cross(k)
-
-    early = chunks // 2
+        issue(k)
+
     for k in range(chunks):
         arrive_near(k)
         give_bufs[k][...] = pick(half_bufs[k], own_ref[...], base * inputs).astype(jnp.bfloat16)
         row_copy(k).start()
 
-    @pl.when(inner == 0)
-    def _():
-        for k in range(early):
-            send_cross(k)
-
-    @pl.when((inner == 0) & (core == 0))
-    def _():
-        for k in range(early, chunks):
-            send_cross(k)
+    issue(ROWS_SENT)
 
     for k in range(chunks):
         row_copy(k).wait_recv()
@@ -416,10 +450,7 @@
 
     loop(0, half, multiply)
 
-    @pl.when((inner == 0) & (core == 1))
-    def _():
-        for k in range(early, chunks):
-            send_cross(k)
+    issue(PRODUCTS_SENT)
 
     feeds = slot_ref.shape[1]
     tile = min(TILE, feeds)

time: 233 us -> 202 us (0.87); the launches traced: 229 us -> 201 us
  Pallas kernels: 228 us -> 200 us
    pallas_call x1, Pallas kernels: 218 us -> 190 us  [split_exchange(): pl.pallas_call(functools.partial(split_kernel, counts, scale), out_shape=...]
where the time goes in v2:
time: 202 us; the launch traced here: 201 us
  Pallas kernels  200 us (99%)
    pallas_call x1, Pallas kernels, split_exchange(): pl.pallas_call(functools.partial(split_kernel, counts, scale), out_shape=...  190 us
    pallas_call x1, Pallas kernels, finish(): pl.pallas_call(functools.partial(kernel, scale), out_shape=jax.ShapeDtype...  9.81 us

profile of v2, /device:TPU:0, one launch (start us, length us, event | category | flops | bytes accessed | tf_op | source)
XLA Modules:
  0.0 201.5 jit_solution(1488093897423325320)
XLA Ops:
  0.0 1.3 dynamic_slice.3
  1.3 190.4 %shard_map.46 = (bf16[16,128,256]{2,1,0:T(8,128)(2,1)}, f32[2,256,4096]{2,1,0:T(8,128)}) custom-call(bf16[96,256]{1,0:T(8,128)(2,1)} %constant.20.clone.bank_ref, s32[519,16,256]{2,1,0:T(8,128)} %bitcast.3, s32[2,16,256]{2,1,0:T(8,128)} %gains_ref.1, s32[1,4096]{1,0:T(1,128)} %bitcast.4, s32[1,256]{1,0:T(1,128)} %bitcast.6), custom_call_target="tpu_custom_call" | custom-call | tf_op jit(solution)/shard_map/pallas_call | solution.py:517
  191.6 9.8 %shard_map.47 = f32[256,2,4096]{2,1,0:T(2,128)} custom-call(bf16[16,128,256]{2,1,0:T(8,128)(2,1)} %get-tuple-element.7.moved_ref, s32[1,4096]{1,0:T(1,128)} %bitcast.5, s32[1,256]{1,0:T(1,128)} %bitcast.7, f32[2,256,4096]{2,1,0:T(8,128)} %get-tuple-element.8.total_ref), custom_call_target="tpu_custom_call" | custom-call | tf_op jit(solution)/shard_map/pallas_call | solution.py:568

commit v3 on v2

--- a/solution.py
+++ b/solution.py
@@ -14,12 +14,14 @@
 SPECTRA = 512
 ROWS = 256
 SHARES = (4, 5, 5, 2)
-SPLIT_SHARES = (2, 3, 2, 1)
+SPLIT_SHARES = (1, 3, 2, 2)
 SPAN = 32
 TILE = 512
 TERMS = 3
 LANES = 128
-ROWS_SENT, PRODUCTS_SENT = 100, 101
+FINISH_TILE = 1024
+UNROLL = 32
+ROWS_SENT, PRODUCTS_SENT, PRODUCTS_HERE = 100, 101, 102
 
 
 def issue_plan():
@@ -269,7 +271,7 @@
         out_ref[:, part, :] = product + total_ref[part]
 
 
-def split_kernel(counts, scale, bank_ref, words_hbm, gains_ref, slot_ref, own_ref, *refs):
+def split_kernel(counts, scale, bank_ref, words_hbm, gains_ref, own_ref, *refs):
     chunks = len(counts)
     refs = list(refs)
 
@@ -278,17 +280,16 @@
         del refs[:count]
         return taken
 
-    last_hbm, total_hbm = take(2)
+    (raw_hbm,) = take(1)
     words_bufs = take(chunks)
     send_bufs = take(chunks)
-    full_bufs = take(chunks - 1)
+    full_bufs = take(chunks)
     half_bufs = take(chunks)
     give_bufs = take(chunks)
     take_bufs = take(chunks)
     lefts = take(chunks)
-    mine, theirs, voltage, rows, total, left = take(6)
-    word_sem, own_sem, total_sem, near_sems, cross_sems, row_sems, product_sems = refs
-    targets = full_bufs + [last_hbm]
+    mine, given, voltage, rows, total, left = take(6)
+    word_sem, own_sem, raw_sem, near_sems, cross_sems, row_sems, product_sems = refs
     me = lax.axis_index("feed")
     size = lax.axis_size("feed")
     half = size // 2
@@ -350,20 +351,20 @@
 
     def far(k, i):
         there = away + (spot + i) % half
-        return remote(send_bufs[k].at[there], targets[k].at[me], cross_sems, (k, half + i), there)
+        return remote(send_bufs[k].at[there], full_bufs[k].at[me], cross_sems, (k, half + i), there)
 
     def close(k, i):
         there = base + (spot + i) % half
-        return remote(send_bufs[k].at[there], targets[k].at[me], cross_sems, (k, i), there)
+        return remote(send_bufs[k].at[there], full_bufs[k].at[me], cross_sems, (k, i), there)
 
     def cross_own(k):
-        return pltpu.make_async_copy(send_bufs[k].at[me], targets[k].at[me], own_sem.at[1, k])
+        return pltpu.make_async_copy(send_bufs[k].at[me], full_bufs[k].at[me], own_sem.at[1, k])
 
     def row_copy(k):
         return remote(give_bufs[k], take_bufs[k], row_sems, k, mate)
 
     def product_copy(j):
-        return remote(mine.at[j], theirs.at[j], product_sems, j, mate)
+        return remote(given.at[j], raw_hbm.at[base + j], product_sems, j, mate)
 
     def send_near(k):
         loop(1, half, lambda d: near(k, d).start())
@@ -436,78 +437,65 @@
         both = give_bufs[k][...].astype(jnp.float32) + take_bufs[k][...].astype(jnp.float32)
         put_left(lefts[k], both, scale)
 
+    def raw_copy(buf, j, slot):
+        return pltpu.make_async_copy(buf.at[slot], raw_hbm.at[j], raw_sem.at[j])
+
     def multiply(j):
         for part in range(2):
             product = None
             for k in range(chunks):
                 term = jnp.dot(lefts[k][part], half_bufs[k][j], preferred_element_type=jnp.float32)
                 product = term if product is None else product + term
-            mine[j, part * ROWS : (part + 1) * ROWS, :] = product.astype(jnp.bfloat16)
+            given[j, part * ROWS : (part + 1) * ROWS, :] = product.astype(jnp.bfloat16)
+
+        @pl.when(core == 0)
+        def _():
+            raw_copy(given, base + j, j).start()
 
         @pl.when(core == 1)
         def _():
             product_copy(j).start()
 
     loop(0, half, multiply)
-
     issue(PRODUCTS_SENT)
-
-    feeds = slot_ref.shape[1]
-    tile = min(TILE, feeds)
 
     @pl.when(core == 0)
     def _():
-        def place_mine(j):
-            where = pl.ds(pl.multiple_of(j * tile, tile), tile)
-            ordered = pick(mine, slot_ref[:, where], base * inputs)
-            total[0, :, where] = ordered[:ROWS]
-            total[1, :, where] = ordered[ROWS:]
-
-        def place_theirs(j):
-            where = pl.ds(pl.multiple_of(j * tile, tile), tile)
-            ordered = pick(theirs, slot_ref[:, where], away * inputs)
-            total[0, :, where] = total[0, :, where] + ordered[:ROWS]
-            total[1, :, where] = total[1, :, where] + ordered[ROWS:]
-
-        loop(0, feeds // tile, place_mine)
+        loop(0, half, lambda j: raw_copy(given, base + j, j).wait())
         loop(0, half, lambda j: product_copy(j).wait_recv())
-        loop(0, feeds // tile, place_theirs)
+        issue(PRODUCTS_HERE)
 
     @pl.when(core == 1)
     def _():
-        for k in range(chunks - 1):
+        for k in range(chunks):
             arrive_cross(k)
             depth = 2 * counts[k]
             set_left(left, full_bufs[k], own_ref[...], scale)
 
-            def columns(j, k=k, depth=depth):
-                where = pl.ds(pl.multiple_of(j * tile, tile), tile)
-                ordered = pick(full_bufs[k], slot_ref[:, where]).astype(jnp.bfloat16)
+            def block(j, k=k, depth=depth):
                 for part in range(2):
-                    product = jnp.dot(left[part, :, :depth], ordered, preferred_element_type=jnp.float32)
+                    rows = slice(part * ROWS, (part + 1) * ROWS)
+                    product = jnp.dot(left[part, :, :depth], full_bufs[k][j], preferred_element_type=jnp.float32)
                     if k:
-                        product = product + total[part, :, where]
-                    total[part, :, where] = product
-
-            loop(0, feeds // tile, columns)
-
-    total_copy = pltpu.make_async_copy(total, total_hbm, total_sem)
-    total_copy.start()
-
-    @pl.when(core == 1)
-    def _():
-        arrive_cross(chunks - 1)
+                        product = product + total[j, rows, :]
+                    if k < chunks - 1:
+                        total[j, rows, :] = product
+                    else:
+                        mine[j, rows, :] = product.astype(jnp.bfloat16)
+                if k == chunks - 1:
+                    raw_copy(mine, j, j).start()
+
+            loop(0, size, block)
+        loop(0, size, lambda j: raw_copy(mine, j, j).wait())
         loop(0, half, lambda j: product_copy(j).wait_send())
 
     for k in range(chunks):
         drain(k)
-    total_copy.wait()
-
-
-def split_exchange(words, gains, feed_slot, own, counts, inputs, scale):
+
+
+def split_exchange(words, gains, own, counts, inputs, scale):
     size = CH
     half = size // 2
-    feeds = feed_slot.shape[0]
     wide = words.shape[2]
     bank = jnp.asarray(filter_bank())
     memory = pl.BlockSpec(memory_space=pltpu.VMEM)
@@ -516,28 +504,25 @@
     half_type = jnp.bfloat16
     return pl.pallas_call(
         functools.partial(split_kernel, counts, scale),
-        out_shape=(
-            jax.ShapeDtypeStruct((size, 2 * counts[-1], inputs), jnp.bfloat16),
-            jax.ShapeDtypeStruct((2, ROWS, feeds), jnp.float32),
-        ),
-        in_specs=[memory, anywhere, memory, memory, memory],
-        out_specs=(anywhere, anywhere),
+        out_shape=jax.ShapeDtypeStruct((size, 2 * ROWS, inputs), half_type),
+        in_specs=[memory, anywhere, memory, memory],
+        out_specs=anywhere,
         scratch_shapes=[pltpu.VMEM((count + TAPS - 1, CH, wide), jnp.int32) for count in counts]
         + [pltpu.VMEM((CH, 2 * count, inputs), half_type) for count in counts]
-        + [pltpu.VMEM((size, 2 * count, inputs), half_type) for count in counts[:-1]]
+        + [pltpu.VMEM((size, 2 * count, inputs), half_type) for count in counts]
         + [pltpu.VMEM((half, 2 * count, inputs), half_type) for count in counts]
         + [pltpu.VMEM((2 * count, ROWS), half_type) for count in counts] * 2
         + [pltpu.VMEM((2, ROWS, 2 * count), half_type) for count in counts]
         + [
-            pltpu.VMEM((half, 2 * ROWS, inputs), half_type),
+            pltpu.VMEM((size, 2 * ROWS, inputs), half_type),
             pltpu.VMEM((half, 2 * ROWS, inputs), half_type),
             pltpu.VMEM(((SPAN + TAPS) * 2 * CH, wide), half_type),
             pltpu.VMEM((2, wide // LANES, SPAN * CH, LANES), jnp.float32),
-            pltpu.VMEM((2, ROWS, feeds), jnp.float32),
+            pltpu.VMEM((size, 2 * ROWS, inputs), jnp.float32),
             pltpu.VMEM((2, ROWS, 2 * max(counts)), half_type),
             pltpu.SemaphoreType.DMA((chunks,)),
             pltpu.SemaphoreType.DMA((2, chunks)),
-            pltpu.SemaphoreType.DMA,
+            pltpu.SemaphoreType.DMA((size,)),
             (pltpu.SemaphoreType.DMA((chunks, half)),) * 2,
             (pltpu.SemaphoreType.DMA((chunks, size)),) * 2,
             (pltpu.SemaphoreType.DMA((chunks,)),) * 2,
@@ -546,27 +531,75 @@
         compiler_params=pltpu.CompilerParams(
             collective_id=0, has_side_effects=True, vmem_limit_bytes=60 * 2**20
         ),
-    )(bank, words, gains, feed_slot[None], own[None])
-
-
-def split_finish_kernel(scale, moved_ref, slot_ref, own_ref, total_ref, out_ref, left):
-    core = lax.axis_index("feed") % 2
-
-    @pl.when(core == 0)
+    )(bank, words, gains, own[None])
+
+
+def turn(block):
+    size = block.shape[1]
+    down = lax.broadcasted_iota(jnp.int32, (size, size), 0)
+    along = lax.broadcasted_iota(jnp.int32, (size, size), 1)
+    same = jnp.where(down == along, 1.0, 0.0).astype(jnp.bfloat16)
+    return lax.dot_general(same, block, (((1,), (1,)), ((), ())), preferred_element_type=jnp.float32)
+
+
+def split_finish_kernel(raw_ref, slot_ref, out_ref, table, picked):
+    sources, depth, width = raw_ref.shape
+    pieces = depth // LANES
+    tile = out_ref.shape[2]
+    first = pl.program_id(0) * tile
+
+    @pl.when(pl.program_id(0) == 0)
     def _():
-        for part in range(2):
-            out_ref[:, part, :] = total_ref[part]
-
-    @pl.when(core == 1)
-    def _():
-        finish_kernel(scale, moved_ref, slot_ref, own_ref, total_ref, out_ref, left)
-
-
-def finish(kernel, moved, feed_slot, own, total, scale):
+        def fill(source, carry):
+            turned = turn(raw_ref[source])
+            for piece in range(pieces):
+                where = pl.ds(source * width * pieces + piece, width, stride=pieces)
+                table[where, :] = turned[:, piece * LANES : (piece + 1) * LANES]
+            return carry
+
+        lax.fori_loop(0, sources, fill, 0)
+
+    def gather(i, carry):
+        for u in range(UNROLL):
+            place = i * UNROLL + u
+            slot = slot_ref[0, first + place]
+            row = table[pl.ds(pl.multiple_of(slot * pieces, pieces), pieces), :]
+            picked[pl.ds(pl.multiple_of(place * pieces, pieces), pieces), :] = row
+        return carry
+
+    lax.fori_loop(0, tile // UNROLL, gather, 0)
+    per = ROWS // LANES
+    for part in range(2):
+        rows = [picked[pl.ds(part * per + piece, tile, stride=pieces), :] for piece in range(per)]
+        out_ref[:, part, :] = turn(jnp.concatenate(rows, axis=1).astype(jnp.bfloat16))
+
+
+def split_finish(raw, feed_slot):
+    sources, depth, width = raw.shape
+    feeds = feed_slot.shape[0]
+    tile = min(FINISH_TILE, feeds)
+    pieces = depth // LANES
+    return pl.pallas_call(
+        split_finish_kernel,
+        out_shape=jax.ShapeDtypeStruct((ROWS, 2, feeds), jnp.float32),
+        grid=(feeds // tile,),
+        in_specs=[
+            pl.BlockSpec(raw.shape, lambda j: (0, 0, 0), pipeline_mode=pl.Buffered(1)),
+            pl.BlockSpec(memory_space=pltpu.SMEM),
+        ],
+        out_specs=pl.BlockSpec((ROWS, 2, tile), lambda j: (0, 0, j)),
+        scratch_shapes=[
+            pltpu.VMEM((sources * width * pieces, LANES), jnp.float32),
+            pltpu.VMEM((tile * pieces, LANES), jnp.float32),
+        ],
+    )(raw, feed_slot[None])
+
+
+def finish(moved, feed_slot, own, total, scale):
     feeds = feed_slot.shape[0]
     tile = min(TILE, feeds)
     return pl.pallas_call(
-        functools.partial(kernel, scale),
+        functools.partial(finish_kernel, scale),
         out_shape=jax.ShapeDtypeStruct((ROWS, 2, feeds), jnp.float32),
         grid=(feeds // tile,),
         in_specs=[
@@ -596,10 +629,10 @@
     own = lax.dynamic_slice_in_dim(feed_slot, first, ROWS, 0)
     scale = 1.0 / spectra
     if split:
-        moved, total = split_exchange(words, gains, feed_slot, own, counts, inputs, scale)
-        return finish(split_finish_kernel, moved, feed_slot, own, total, scale)
+        raw = split_exchange(words, gains, own, counts, inputs, scale)
+        return split_finish(raw, feed_slot)
     moved, total = exchange(words, gains, feed_slot, own, counts, inputs, groups, scale)
-    return finish(finish_kernel, moved, feed_slot, own, total, scale)
+    return finish(moved, feed_slot, own, total, scale)
 
 
 def solution(mesh):

time: 202 us -> 195 us (0.965)
  Pallas kernels: 200 us -> 193 us
    pallas_call x1, Pallas kernels: 190 us -> 177 us  [split_exchange(): pl.pallas_call(functools.partial(split_kernel, counts, scale), out_shape=...]
    pallas_call x1, Pallas kernels: 9.81 us -> 16.4 us  [split_finish(): pl.pallas_call(split_finish_kernel, out_shape=jax.ShapeDtypeStruct((ROWS,...]
where the time goes in v3:
time: 195 us
  Pallas kernels  193 us (99%)
    pallas_call x1, Pallas kernels, split_exchange(): pl.pallas_call(functools.partial(split_kernel, counts, scale), out_shape=...  177 us
    pallas_call x1, Pallas kernels, split_finish(): pl.pallas_call(split_finish_kernel, out_shape=jax.ShapeDtypeStruct((ROWS,...  16.4 us

profile of v3, /device:TPU:0, one launch (start us, length us, event | category | flops | bytes accessed | tf_op | source)
XLA Modules:
  0.0 194.6 jit_solution(8464883298078340294)
XLA Ops:
  0.0 1.2 dynamic_slice.3
  1.2 177.0 %shard_map.46.raw_ref = bf16[16,512,256]{2,1,0:T(8,128)(2,1)} custom-call(bf16[96,256]{1,0:T(8,128)(2,1)} %constant.20.clone.bank_ref, s32[519,16,256]{2,1,0:T(8,128)} %bitcast.3, s32[2,16,256]{2,1,0:T(8,128)} %gains_ref.1, s32[1,256]{1,0:T(1,128)} %bitcast.5), custom_call_target="tpu_custom_call" | custom-call | tf_op jit(solution)/shard_map/pallas_call | solution.py:505
  178.2 16.4 %shard_map.47 = f32[256,2,4096]{2,1,0:T(2,128)} custom-call(bf16[16,512,256]{2,1,0:T(8,128)(2,1)} %shard_map.46.raw_ref, s32[1,4096]{1,0:T(1,128)} %bitcast.4), custom_call_target="tpu_custom_call" | custom-call | tf_op jit(solution)/shard_map/pallas_call | solution.py:582

commit v4 on v3

--- a/solution.py
+++ b/solution.py
@@ -20,8 +20,8 @@
 TERMS = 3
 LANES = 128
 FINISH_TILE = 1024
-UNROLL = 32
-ROWS_SENT, PRODUCTS_SENT, PRODUCTS_HERE = 100, 101, 102
+STEP = 256
+ROWS_SENT, PRODUCTS_SENT, PRODUCTS_HERE, ROW_STAGE = 100, 101, 102, 200
 
 
 def issue_plan():
@@ -34,7 +34,7 @@
         inner += [(PRODUCTS_SENT if core else ROWS_SENT, "close", k) for k in chunks]
         outer = []
         for k in chunks:
-            stage = last if k < 2 - core else PRODUCTS_SENT if core else ROWS_SENT
+            stage = ROW_STAGE + k if k < 2 - core else PRODUCTS_SENT if core else ROWS_SENT
             outer += [(stage, kind, k) for kind in kinds]
         plan[2 + core] = inner
         plan[core] = outer
@@ -271,7 +271,7 @@
         out_ref[:, part, :] = product + total_ref[part]
 
 
-def split_kernel(counts, scale, bank_ref, words_hbm, gains_ref, own_ref, *refs):
+def split_kernel(counts, scale, bank_ref, words_hbm, gains_ref, slot_ref, *refs):
     chunks = len(counts)
     refs = list(refs)
 
@@ -302,6 +302,7 @@
     inner = (quarter + 1) // 2 % 2
     inputs = send_bufs[0].shape[2]
     bank = bank_ref[...]
+    own = slot_ref[:, :ROWS]
     gain = gains_ref[...].astype(jnp.float32) * (1.0 / 2048.0)
 
     barrier = pltpu.get_barrier_semaphore()
@@ -427,8 +428,9 @@
 
     for k in range(chunks):
         arrive_near(k)
-        give_bufs[k][...] = pick(half_bufs[k], own_ref[...], base * inputs).astype(jnp.bfloat16)
+        give_bufs[k][...] = pick(half_bufs[k], own, base * inputs).astype(jnp.bfloat16)
         row_copy(k).start()
+        issue(ROW_STAGE + k)
 
     issue(ROWS_SENT)
 
@@ -470,7 +472,7 @@
         for k in range(chunks):
             arrive_cross(k)
             depth = 2 * counts[k]
-            set_left(left, full_bufs[k], own_ref[...], scale)
+            set_left(left, full_bufs[k], own, scale)
 
             def block(j, k=k, depth=depth):
                 for part in range(2):
@@ -493,7 +495,7 @@
         drain(k)
 
 
-def split_exchange(words, gains, own, counts, inputs, scale):
+def split_exchange(words, gains, feed_slot, counts, inputs, scale):
     size = CH
     half = size // 2
     wide = words.shape[2]
@@ -531,7 +533,7 @@
         compiler_params=pltpu.CompilerParams(
             collective_id=0, has_side_effects=True, vmem_limit_bytes=60 * 2**20
         ),
-    )(bank, words, gains, own[None])
+    )(bank, words, gains, feed_slot[None])
 
 
 def turn(block):
@@ -542,55 +544,72 @@
     return lax.dot_general(same, block, (((1,), (1,)), ((), ())), preferred_element_type=jnp.float32)
 
 
-def split_finish_kernel(raw_ref, slot_ref, out_ref, table, picked):
-    sources, depth, width = raw_ref.shape
+def split_finish_kernel(raw_hbm, slot_ref, out_ref, raw, table, even, odd, sems):
+    sources, depth, width = raw.shape
     pieces = depth // LANES
+    per = ROWS // LANES
     tile = out_ref.shape[2]
     first = pl.program_id(0) * tile
+    step = even.shape[0] // pieces
+
+    def raw_copy(source):
+        return pltpu.make_async_copy(raw_hbm.at[source], raw.at[source], sems.at[source])
 
     @pl.when(pl.program_id(0) == 0)
     def _():
+        def begin(source, carry):
+            raw_copy(source).start()
+            return carry
+
         def fill(source, carry):
-            turned = turn(raw_ref[source])
+            raw_copy(source).wait()
+            turned = turn(raw[source])
             for piece in range(pieces):
                 where = pl.ds(source * width * pieces + piece, width, stride=pieces)
                 table[where, :] = turned[:, piece * LANES : (piece + 1) * LANES]
             return carry
 
+        lax.fori_loop(0, sources, begin, 0)
         lax.fori_loop(0, sources, fill, 0)
 
-    def gather(i, carry):
-        for u in range(UNROLL):
-            place = i * UNROLL + u
-            slot = slot_ref[0, first + place]
+    def gather(picked, begin):
+        for place in range(step):
+            slot = slot_ref[0, first + begin + place]
             row = table[pl.ds(pl.multiple_of(slot * pieces, pieces), pieces), :]
-            picked[pl.ds(pl.multiple_of(place * pieces, pieces), pieces), :] = row
-        return carry
-
-    lax.fori_loop(0, tile // UNROLL, gather, 0)
-    per = ROWS // LANES
-    for part in range(2):
-        rows = [picked[pl.ds(part * per + piece, tile, stride=pieces), :] for piece in range(per)]
-        out_ref[:, part, :] = turn(jnp.concatenate(rows, axis=1).astype(jnp.bfloat16))
+            picked[place * pieces : (place + 1) * pieces, :] = row
+
+    def put(picked, begin):
+        for part in range(2):
+            rows = [picked[pl.ds(part * per + piece, step, stride=pieces), :] for piece in range(per)]
+            turned = turn(jnp.concatenate(rows, axis=1).astype(jnp.bfloat16))
+            out_ref[:, part, begin : begin + step] = turned
+
+    gather(even, 0)
+    for i in range(tile // step):
+        here, there = (even, odd) if i % 2 == 0 else (odd, even)
+        if i + 1 < tile // step:
+            gather(there, (i + 1) * step)
+        put(here, i * step)
 
 
 def split_finish(raw, feed_slot):
     sources, depth, width = raw.shape
     feeds = feed_slot.shape[0]
     tile = min(FINISH_TILE, feeds)
+    step = min(STEP, tile)
     pieces = depth // LANES
     return pl.pallas_call(
         split_finish_kernel,
         out_shape=jax.ShapeDtypeStruct((ROWS, 2, feeds), jnp.float32),
         grid=(feeds // tile,),
-        in_specs=[
-            pl.BlockSpec(raw.shape, lambda j: (0, 0, 0), pipeline_mode=pl.Buffered(1)),
-            pl.BlockSpec(memory_space=pltpu.SMEM),
-        ],
+        in_specs=[pl.BlockSpec(memory_space=pl.ANY), pl.BlockSpec(memory_space=pltpu.SMEM)],
         out_specs=pl.BlockSpec((ROWS, 2, tile), lambda j: (0, 0, j)),
         scratch_shapes=[
+            pltpu.VMEM(raw.shape, raw.dtype),
             pltpu.VMEM((sources * width * pieces, LANES), jnp.float32),
-            pltpu.VMEM((tile * pieces, LANES), jnp.float32),
+            pltpu.VMEM((step * pieces, LANES), jnp.float32),
+            pltpu.VMEM((step * pieces, LANES), jnp.float32),
+            pltpu.SemaphoreType.DMA((sources,)),
         ],
     )(raw, feed_slot[None])
 
@@ -626,11 +645,11 @@
     if spare:
         words = jnp.pad(words, ((0, 0), (0, 0), (0, spare)))
         gains = jnp.pad(gains, ((0, 0), (0, 0), (0, spare)))
-    own = lax.dynamic_slice_in_dim(feed_slot, first, ROWS, 0)
     scale = 1.0 / spectra
     if split:
-        raw = split_exchange(words, gains, own, counts, inputs, scale)
+        raw = split_exchange(words, gains, feed_slot, counts, inputs, scale)
         return split_finish(raw, feed_slot)
+    own = lax.dynamic_slice_in_dim(feed_slot, first, ROWS, 0)
     moved, total = exchange(words, gains, feed_slot, own, counts, inputs, groups, scale)
     return finish(moved, feed_slot, own, total, scale)
 

time: 195 us -> 193 us (0.990)
  no operation moved by 1% of the time
where the time goes in v4:
time: 193 us; the launch traced here: 192 us
  Pallas kernels  192 us (99%)
    pallas_call x1, Pallas kernels, split_exchange(): pl.pallas_call(functools.partial(split_kernel, counts, scale), out_shape=...  177 us
    pallas_call x1, Pallas kernels, split_finish(): pl.pallas_call(split_finish_kernel, out_shape=jax.ShapeDtypeStruct((ROWS,...  15 us

profile of v4, /device:TPU:0, one launch (start us, length us, event | category | flops | bytes accessed | tf_op | source)
XLA Modules:
  0.0 192.2 jit_solution(15141155461829213644)
XLA Ops:
  0.0 177.1 %shard_map.46.raw_hbm = bf16[16,512,256]{2,1,0:T(8,128)(2,1)} custom-call(bf16[96,256]{1,0:T(8,128)(2,1)} %constant.2.clone.bank_ref, s32[519,16,256]{2,1,0:T(8,128)} %bitcast.2, s32[2,16,256]{2,1,0:T(8,128)} %gains_ref.1, s32[1,4096]{1,0:T(1,128)} %bitcast.3), custom_call_target="tpu_custom_call" | custom-call | tf_op jit(solution)/shard_map/pallas_call | solution.py:507
  177.1 15.0 %shard_map.47 = f32[256,2,4096]{2,1,0:T(2,128)} custom-call(bf16[16,512,256]{2,1,0:T(8,128)(2,1)} %shard_map.46.raw_hbm, s32[1,4096]{1,0:T(1,128)} %bitcast.4), custom_call_target="tpu_custom_call" | custom-call | tf_op jit(solution)/shard_map/pallas_call | solution.py:601

commit v5 on v4

--- a/solution.py
+++ b/solution.py
@@ -20,7 +20,7 @@
 TERMS = 3
 LANES = 128
 FINISH_TILE = 1024
-STEP = 256
+STEP = 512
 ROWS_SENT, PRODUCTS_SENT, PRODUCTS_HERE, ROW_STAGE = 100, 101, 102, 200
 
 
@@ -416,10 +416,11 @@
         loop(1, half, lambda i: close(k, i).wait_recv())
         loop(0, half, lambda i: far(k, i).wait_recv())
 
-    for k in range(chunks):
-        word_copy(k).start()
+    word_copy(0).start()
     for k in range(chunks):
         word_copy(k).wait()
+        if k + 1 < chunks:
+            word_copy(k + 1).start()
         channelize(counts[k], bank, gain, words_bufs[k], send_bufs[k], voltage, rows)
         if k == 0:
             pl.semaphore_wait(barrier, size - 1)

time: 193 us -> 191 us (0.990)
  no operation moved by 1% of the time
where the time goes in v5:
time: 191 us
  Pallas kernels  191 us (100%)
    pallas_call x1, Pallas kernels, split_exchange(): pl.pallas_call(functools.partial(split_kernel, counts, scale), out_shape=...  177 us
    pallas_call x1, Pallas kernels, split_finish(): pl.pallas_call(split_finish_kernel, out_shape=jax.ShapeDtypeStruct((ROWS,...  13.9 us

profile of v5, /device:TPU:0, one launch (start us, length us, event | category | flops | bytes accessed | tf_op | source)
XLA Modules:
  0.0 191.0 jit_solution(18182530461073986245)
XLA Ops:
  0.0 177.1 %shard_map.46.raw_hbm = bf16[16,512,256]{2,1,0:T(8,128)(2,1)} custom-call(bf16[96,256]{1,0:T(8,128)(2,1)} %constant.2.clone.bank_ref, s32[519,16,256]{2,1,0:T(8,128)} %bitcast.2, s32[2,16,256]{2,1,0:T(8,128)} %gains_ref.1, s32[1,4096]{1,0:T(1,128)} %bitcast.3), custom_call_target="tpu_custom_call" | custom-call | tf_op jit(solution)/shard_map/pallas_call | solution.py:508
  177.1 13.9 %shard_map.47 = f32[256,2,4096]{2,1,0:T(2,128)} custom-call(bf16[16,512,256]{2,1,0:T(8,128)(2,1)} %shard_map.46.raw_hbm, s32[1,4096]{1,0:T(1,128)} %bitcast.4), custom_call_target="tpu_custom_call" | custom-call | tf_op jit(solution)/shard_map/pallas_call | solution.py:602

commit v6 on v5

--- a/solution.py
+++ b/solution.py
@@ -25,13 +25,13 @@
 
 
 def issue_plan():
-    kinds = ("straight", "across", "close")
+    kinds = ("across", "straight", "close")
     chunks = range(len(SPLIT_SHARES))
     last = chunks[-1]
     plan = {}
     for core in range(2):
         inner = [(k, "straight", k) for k in chunks] + [(last, "across", k) for k in chunks]
-        inner += [(PRODUCTS_SENT if core else ROWS_SENT, "close", k) for k in chunks]
+        inner += [(ROWS_SENT, "close", k) for k in chunks]
         outer = []
         for k in chunks:
             stage = ROW_STAGE + k if k < 2 - core else PRODUCTS_SENT if core else ROWS_SENT

time: 191 us -> 191 us (level)
  no operation moved by 1% of the time
where the time goes in v6:
time: 191 us
  Pallas kernels  191 us (100%)
    pallas_call x1, Pallas kernels, split_exchange(): pl.pallas_call(functools.partial(split_kernel, counts, scale), out_shape=...  177 us
    pallas_call x1, Pallas kernels, split_finish(): pl.pallas_call(split_finish_kernel, out_shape=jax.ShapeDtypeStruct((ROWS,...  13.9 us

profile of v6, /device:TPU:0, one launch (start us, length us, event | category | flops | bytes accessed | tf_op | source)
XLA Modules:
  0.0 191.0 jit_solution(3869437647269160588)
XLA Ops:
  0.0 177.1 %shard_map.46.raw_hbm = bf16[16,512,256]{2,1,0:T(8,128)(2,1)} custom-call(bf16[96,256]{1,0:T(8,128)(2,1)} %constant.2.clone.bank_ref, s32[519,16,256]{2,1,0:T(8,128)} %bitcast.2, s32[2,16,256]{2,1,0:T(8,128)} %gains_ref.1, s32[1,4096]{1,0:T(1,128)} %bitcast.3), custom_call_target="tpu_custom_call" | custom-call | tf_op jit(solution)/shard_map/pallas_call | solution.py:508
  177.1 13.9 %shard_map.47 = f32[256,2,4096]{2,1,0:T(2,128)} custom-call(bf16[16,512,256]{2,1,0:T(8,128)(2,1)} %shard_map.46.raw_hbm, s32[1,4096]{1,0:T(1,128)} %bitcast.4), custom_call_target="tpu_custom_call" | custom-call | tf_op jit(solution)/shard_map/pallas_call | solution.py:602
